TPU v7x, 32 devices: a whole 2x2x4 slice. The times are simulated.
32 devices in a mesh: seq: 8 (over z, y), tok: 4 (over x, core).
Axes of the slice: x: 2, y: 2, z: 4, core: 2. Of those that a mesh axis runs over, the one named last changes fastest.
Arguments:
- tokens: bfloat16 [8, 1024, 1024], P('seq', 'tok'), may hold values from -6 to 6
- out_grad: bfloat16 [8, 1024, 1024], P('seq', 'tok'), may hold values from -6 to 6
- segments: int32 [8, 1024], P('seq'), may hold values from 0 to 2, never falling along the last dimension, each value on 1 to 512 neighbouring positions
- adapter_index: int32 [8], P('seq'), may hold values from 0 to 7
- qkv_weight: bfloat16 [1024, 3072], P('tok', 'seq'), may hold values from -0.1875 to 0.1875
- out_weight: bfloat16 [1024, 1024], P('tok', 'seq'), may hold values from -0.75 to 0.75
- in_weight: bfloat16 [1024, 5248], P('tok', 'seq'), may hold values from -0.1875 to 0.1875
- out2_weight: bfloat16 [2624, 1024], P('tok', 'seq'), may hold values from -0.15625 to 0.15625
- attn_gain: bfloat16 [1024], P('tok'), may hold values from 0.099609375 to 1.8984375
- mlp_gain: bfloat16 [1024], P('tok'), may hold values from 0.099609375 to 1.8984375
- qkv_down: bfloat16 [8, 16, 1024], replicated, may hold values from -0.1875 to 0.1875
- qkv_up: bfloat16 [8, 16, 3072], replicated, may hold values from -0.5 to 0.5
- out_down: bfloat16 [8, 16, 1024], replicated, may hold values from -0.1875 to 0.1875
- out_up: bfloat16 [8, 16, 1024], replicated, may hold values from -1.5 to 1.5
- in_down: bfloat16 [8, 16, 1024], replicated, may hold values from -0.1875 to 0.1875
- in_up: bfloat16 [8, 16, 5248], replicated, may hold values from -0.5 to 0.5
- out2_down: bfloat16 [8, 16, 2624], replicated, may hold values from -0.125 to 0.125
- out2_up: bfloat16 [8, 16, 1024], replicated, may hold values from -0.5 to 0.5
Outputs:
- layer_out: bfloat16 [8, 1024, 1024], P('seq', 'tok')
- input_grad: bfloat16 [8, 1024, 1024], P('seq', 'tok')
- qkv_down_grad: float32 [8, 16, 1024], replicated
- qkv_up_grad: float32 [8, 16, 3072], replicated
- out_down_grad: float32 [8, 16, 1024], replicated
- out_up_grad: float32 [8, 16, 1024], replicated
- in_down_grad: float32 [8, 16, 1024], replicated
- in_up_grad: float32 [8, 16, 5248], replicated
- out2_down_grad: float32 [8, 16, 2624], replicated
- out2_up_grad: float32 [8, 16, 1024], replicated
Inputs may be any that keep to these rules, and one draw needn't show every extreme that they name: `segments`: within a sequence the document numbers never fall; each document has 1 to 512 tokens, one of each sequence exactly 512.
All inputs are finite; a program needn't handle non-finite values.
Results may differ from a plain program's by a relative error of at most 0.018.
Values may be sent and summed in bfloat16 or wider, within the bound.
No kernel may reach another device: no remote copies, remote signals or barrier semaphores. Data moves between devices by JAX's collectives and lax.ppermute only.
A program may use at most 128 MiB of HBM per device.

v0:
```python
import jax
import jax.numpy as jnp
from jax import lax
from jax.sharding import PartitionSpec as P

HEADS = 16
HEAD_DIM = 64
FF = 2624
ADAPTERS = 8
EPS = 1e-05
THETA = 160000.0
HIGH = lax.Precision.HIGHEST


def layer_norm(values, gain_vec):
    middle = jnp.mean(values, axis=-1, keepdims=True)
    centered = values - middle
    spread = jnp.mean(centered * centered, axis=-1, keepdims=True)
    return centered * lax.rsqrt(spread + EPS) * gain_vec


def rotary_table(positions, head_width):
    exponent = jnp.arange(0, head_width, 2).astype(jnp.float32) / head_width
    inverse = 1.0 / THETA**exponent
    phases = positions.astype(jnp.float32)[:, None] * inverse[None, :]
    cosine = jnp.concatenate([jnp.cos(phases), jnp.cos(phases)], -1)
    sine_part = jnp.concatenate([jnp.sin(phases), jnp.sin(phases)], -1)
    return (cosine, sine_part)


def rotary(values, cosine, sine_part):
    half_width = values.shape[-1] // 2
    turned = jnp.concatenate([-values[..., half_width:], values[..., :half_width]], -1)
    return values * cosine[None, :, None, :] + turned * sine_part[None, :, None, :]


def glu_act(inputs, gate_vals):
    return jax.nn.gelu(inputs, approximate=False) * gate_vals


def select(table_rows, onehot_low):
    return jnp.einsum(
        "sa,ayz->syz", onehot_low, table_rows, preferred_element_type=jnp.float32
    ).astype(jnp.bfloat16)


def spread_back(term_rows, onehot):
    return jnp.einsum(
        "sa,syz->ayz", onehot, term_rows, precision=HIGH, preferred_element_type=jnp.float32
    )


def project(inputs, weight, down_rows, up_rows):
    seq_count, row_count, width_in = inputs.shape
    main_part = jnp.dot(
        inputs.reshape(seq_count * row_count, width_in), weight, preferred_element_type=jnp.float32
    )
    narrow = jnp.einsum(
        "std,srd->str", inputs, down_rows, preferred_element_type=jnp.float32
    ).astype(jnp.bfloat16)
    extra_part = jnp.einsum("str,sre->ste", narrow, up_rows, preferred_element_type=jnp.float32)
    return (main_part.reshape(seq_count, row_count, -1) + extra_part, narrow)


def project_back(grad_out, inputs, narrow, weight, down_rows, up_rows):
    seq_count, row_count, width_out = grad_out.shape
    main_part = lax.dot_general(
        grad_out.reshape(seq_count * row_count, width_out),
        weight,
        (((1,), (1,)), ((), ())),
        preferred_element_type=jnp.float32,
    )
    inner_grad = jnp.einsum(
        "ste,sre->str", grad_out, up_rows, preferred_element_type=jnp.float32
    ).astype(jnp.bfloat16)
    back_sum = main_part.reshape(seq_count, row_count, -1) + jnp.einsum(
        "str,srd->std", inner_grad, down_rows, preferred_element_type=jnp.float32
    )
    grad_up = jnp.einsum("str,ste->sre", narrow, grad_out, preferred_element_type=jnp.float32)
    grad_down = jnp.einsum("str,std->srd", inner_grad, inputs, preferred_element_type=jnp.float32)
    return (back_sum, grad_down, grad_up)


def masked_scores(query_part, key_part, doc_mask):
    scores = (
        jnp.einsum("sqhd,skhd->shqk", query_part, key_part, preferred_element_type=jnp.float32)
        * 0.125
    )
    return jnp.where(doc_mask[:, None, :, :], scores, -1e30)


def heads_slice(source, group_index, group_width, head_width):
    part_cols = lax.dynamic_slice_in_dim(source, group_index * group_width, group_width, 2)
    return part_cols.reshape(
        part_cols.shape[0], part_cols.shape[1], group_width // head_width, head_width
    )


def join_groups(parts):
    moved = jnp.moveaxis(parts, 0, 2)
    return moved.reshape(moved.shape[0], moved.shape[1], -1)


def body(
    tokens,
    out_grad,
    segments,
    adapter_index,
    qkv_weight,
    out_weight,
    in_weight,
    out2_weight,
    attn_gain,
    mlp_gain,
    qkv_down,
    qkv_up,
    out_down,
    out_up,
    in_down,
    in_up,
    out2_down,
    out2_up,
):
    seq_count, tok_rows, model_width = tokens.shape
    head_width = HEAD_DIM
    group_width = 2 * head_width
    groups = jnp.arange(HEADS // 2)
    seq_length = segments.shape[1]
    tok_start = lax.axis_index("tok") * tok_rows
    positions = tok_start + jnp.arange(tok_rows)
    cosine, sine_part = rotary_table(positions, head_width)
    own_segments = lax.dynamic_slice_in_dim(segments, tok_start, tok_rows, 1)
    doc_mask = own_segments[:, :, None] == segments[:, None, :]
    pick_bits = adapter_index[:, None] == jnp.arange(ADAPTERS)[None, :]
    onehot = pick_bits.astype(jnp.float32)
    onehot_low = pick_bits.astype(jnp.bfloat16)
    picked = [
        select(table_rows, onehot_low)
        for table_rows in (qkv_down, qkv_up, out_down, out_up, in_down, in_up, out2_down, out2_up)
    ]
    tok_parts = (
        lax.all_gather(qkv_weight, "tok", axis=0, tiled=True),
        lax.all_gather(out_weight, "tok", axis=0, tiled=True),
        lax.all_gather(in_weight, "tok", axis=0, tiled=True),
        lax.all_gather(out2_weight, "tok", axis=0, tiled=True),
        lax.all_gather(attn_gain, "tok", axis=0, tiled=True),
        lax.all_gather(mlp_gain, "tok", axis=0, tiled=True),
    )
    w_qkv, w_out, w_in, w_out2 = (
        lax.all_gather(tok_parts[0], "seq", axis=1, tiled=True),
        lax.all_gather(tok_parts[1], "seq", axis=1, tiled=True),
        lax.all_gather(tok_parts[2], "seq", axis=1, tiled=True),
        lax.all_gather(tok_parts[3], "seq", axis=1, tiled=True),
    )
    gain_one = tok_parts[4].astype(jnp.float32)
    gain_two = tok_parts[5].astype(jnp.float32)
    inputs = tokens.astype(jnp.float32)
    norm_one = layer_norm(inputs, gain_one).astype(jnp.bfloat16)
    qkv, narrow_qkv = project(norm_one, w_qkv, picked[0], picked[1])
    head_shape = (seq_count, tok_rows, HEADS, head_width)
    query_pre = qkv[..., :model_width].reshape(head_shape)
    query_low = (
        rotary(query_pre, cosine, sine_part)
        .reshape(seq_count, tok_rows, model_width)
        .astype(jnp.bfloat16)
    )
    key_low = (
        rotary(qkv[..., model_width : 2 * model_width].reshape(head_shape), cosine, sine_part)
        .reshape(seq_count, tok_rows, model_width)
        .astype(jnp.bfloat16)
    )
    value_low = qkv[..., 2 * model_width :].astype(jnp.bfloat16)
    keys_all, values_all = (
        lax.all_gather(key_low, "tok", axis=1, tiled=True),
        lax.all_gather(value_low, "tok", axis=1, tiled=True),
    )

    def forward_group(group_index):
        query_part = heads_slice(query_low, group_index, group_width, head_width)
        key_part = heads_slice(keys_all, group_index, group_width, head_width)
        value_part = heads_slice(values_all, group_index, group_width, head_width)
        scores = masked_scores(query_part, key_part, doc_mask)
        row_max = jnp.max(scores, axis=-1, keepdims=True)
        row_total = jnp.sum(jnp.exp(scores - row_max), axis=-1, keepdims=True)
        log_total = row_max + jnp.log(row_total)
        attn_prob = jnp.exp(scores - log_total).astype(jnp.bfloat16)
        mixed = jnp.einsum(
            "shqk,skhd->sqhd", attn_prob, value_part, preferred_element_type=jnp.float32
        )
        return (mixed.reshape(seq_count, tok_rows, group_width), log_total[..., 0])

    mixed_parts, log_totals = lax.map(forward_group, groups)
    attn_low = join_groups(mixed_parts).astype(jnp.bfloat16)
    attn_branch, narrow_out = project(attn_low, w_out, picked[2], picked[3])
    middle = inputs + attn_branch
    norm_two = layer_norm(middle, gain_two).astype(jnp.bfloat16)
    gate_up, narrow_in = project(norm_two, w_in, picked[4], picked[5])
    act_low = glu_act(gate_up[..., :FF], gate_up[..., FF:]).astype(jnp.bfloat16)
    mlp_branch, narrow_out2 = project(act_low, w_out2, picked[6], picked[7])
    layer_out = (middle + mlp_branch).astype(jnp.bfloat16)
    back_parts = (
        lax.all_gather(qkv_weight, "tok", axis=0, tiled=True),
        lax.all_gather(out_weight, "tok", axis=0, tiled=True),
        lax.all_gather(in_weight, "tok", axis=0, tiled=True),
        lax.all_gather(out2_weight, "tok", axis=0, tiled=True),
    )
    w_qkv, w_out, w_in, w_out2 = (
        lax.all_gather(back_parts[0], "seq", axis=1, tiled=True),
        lax.all_gather(back_parts[1], "seq", axis=1, tiled=True),
        lax.all_gather(back_parts[2], "seq", axis=1, tiled=True),
        lax.all_gather(back_parts[3], "seq", axis=1, tiled=True),
    )
    grad_y = out_grad.astype(jnp.float32)
    back_act, down_o2, up_o2 = project_back(
        out_grad, act_low, narrow_out2, w_out2, picked[6], picked[7]
    )
    _, glu_back = jax.vjp(glu_act, gate_up[..., :FF], gate_up[..., FF:])
    grad_in, grad_gate = glu_back(back_act)
    grad_z = jnp.concatenate([grad_in, grad_gate], axis=-1).astype(jnp.bfloat16)
    back_norm_two, down_in, up_in = project_back(
        grad_z, norm_two, narrow_in, w_in, picked[4], picked[5]
    )
    _, norm_two_back = jax.vjp(lambda field: layer_norm(field, gain_two), middle)
    grad_mid = grad_y + norm_two_back(back_norm_two)[0]
    grad_a = grad_mid.astype(jnp.bfloat16)
    back_attn, down_out, up_out = project_back(
        grad_a, attn_low, narrow_out, w_out, picked[2], picked[3]
    )
    grad_attn = back_attn.astype(jnp.bfloat16)

    def query_grads(group_index):
        query_part = heads_slice(query_low, group_index, group_width, head_width)
        key_part = heads_slice(keys_all, group_index, group_width, head_width)
        value_part = heads_slice(values_all, group_index, group_width, head_width)
        grad_part = heads_slice(grad_attn, group_index, group_width, head_width)
        scores = masked_scores(query_part, key_part, doc_mask)
        attn_prob = jnp.exp(scores - log_totals[group_index][..., None])
        grad_prob = jnp.einsum(
            "sqhd,skhd->shqk", grad_part, value_part, preferred_element_type=jnp.float32
        )
        row_dot = jnp.sum(attn_prob * grad_prob, axis=-1)
        grad_scores = (attn_prob * (grad_prob - row_dot[..., None]) * 0.125).astype(jnp.bfloat16)
        grad_query = jnp.einsum(
            "shqk,skhd->sqhd", grad_scores, key_part, preferred_element_type=jnp.float32
        )
        return (
            query_part,
            grad_part,
            attn_prob,
            grad_scores,
            grad_query.reshape(seq_count, tok_rows, group_width),
            row_dot,
        )

    def summed_group(group_index):
        query_part, grad_part, attn_prob, grad_scores, grad_query, row_dot = query_grads(
            group_index
        )
        grad_key = jnp.einsum(
            "shqk,sqhd->skhd", grad_scores, query_part, preferred_element_type=jnp.float32
        )
        grad_value = jnp.einsum(
            "shqk,sqhd->skhd",
            attn_prob.astype(jnp.bfloat16),
            grad_part,
            preferred_element_type=jnp.float32,
        )
        grad_key, grad_value = (
            lax.psum_scatter(
                grad_key.reshape(seq_count, seq_length, group_width).astype(jnp.bfloat16),
                "tok",
                scatter_dimension=1,
                tiled=True,
            ).astype(jnp.float32),
            lax.psum_scatter(
                grad_value.reshape(seq_count, seq_length, group_width).astype(jnp.bfloat16),
                "tok",
                scatter_dimension=1,
                tiled=True,
            ).astype(jnp.float32),
        )
        return (grad_query, grad_key, grad_value)

    query_parts, key_parts, value_parts = lax.map(summed_group, groups)
    grad_query = join_groups(query_parts)
    grad_key = join_groups(key_parts)
    grad_value = join_groups(value_parts)
    _, rotate_back = jax.vjp(lambda field: rotary(field, cosine, sine_part), query_pre)
    grad_query_pre = rotate_back(grad_query.reshape(head_shape))[0].reshape(
        seq_count, tok_rows, model_width
    )
    grad_key_pre = rotate_back(grad_key.reshape(head_shape))[0].reshape(
        seq_count, tok_rows, model_width
    )
    grad_qkv = jnp.concatenate([grad_query_pre, grad_key_pre, grad_value], axis=-1).astype(
        jnp.bfloat16
    )
    back_norm_one, down_qkv, up_qkv = project_back(
        grad_qkv, norm_one, narrow_qkv, w_qkv, picked[0], picked[1]
    )
    _, norm_one_back = jax.vjp(lambda field: layer_norm(field, gain_one), inputs)
    input_grad = (grad_mid + norm_one_back(back_norm_one)[0]).astype(jnp.bfloat16)
    terms = (down_qkv, up_qkv, down_out, up_out, down_in, up_in, down_o2, up_o2)
    summed = lax.psum(
        (
            spread_back(terms[0], onehot),
            spread_back(terms[1], onehot),
            spread_back(terms[2], onehot),
            spread_back(terms[3], onehot),
            spread_back(terms[4], onehot),
            spread_back(terms[5], onehot),
            spread_back(terms[6], onehot),
            spread_back(terms[7], onehot),
        ),
        ("seq", "tok"),
    )
    return (
        layer_out,
        input_grad,
        summed[0],
        summed[1],
        summed[2],
        summed[3],
        summed[4],
        summed[5],
        summed[6],
        summed[7],
    )


def solution(mesh):
    return jax.shard_map(
        body,
        mesh=mesh,
        in_specs=(
            P("seq", "tok", None),
            P("seq", "tok", None),
            P("seq", None),
            P("seq"),
            P("tok", "seq"),
            P("tok", "seq"),
            P("tok", "seq"),
            P("tok", "seq"),
            P("tok"),
            P("tok"),
            P(),
            P(),
            P(),
            P(),
            P(),
            P(),
            P(),
            P(),
        ),
        out_specs=(
            P("seq", "tok", None),
            P("seq", "tok", None),
            P(),
            P(),
            P(),
            P(),
            P(),
            P(),
            P(),
            P(),
        ),
        check_vma=False,
    )
```

profile of v0, /device:TPU:0, one launch (start us, length us, event | category | flops | bytes accessed | tf_op | source)
XLA Modules:
  0.0 1193.3 jit_solution(8519961414103918297)
XLA Ops:
  7.3 11.8 all_gather.45
  44.1 75.4 %all-gather.10.cloned.1.call-done = bf16[1024,3072]{1,0:T(8,128)(2,1)} async-done(((bf16[1024,384]{1,0:T(8,128)(2,1)}), bf16[1024,3072]{1,0:T(8,128)(2,1)}) %all-gather.10.cloned.1.call-update) | async-done | bytes 6291472 | tf_op jit(solution)/shard_map/all_gather | solution.py:150
  169.6 59.1 %all-gather.22.cloned.1.call-done = bf16[2624,1024]{1,0:T(8,128)(2,1)} async-done(((bf16[2624,128]{1,0:T(8,128)(2,1)}), bf16[2624,1024]{1,0:T(8,128)(2,1)}) %all-gather.22.cloned.1.call-update) | async-done | bytes 5373968 | tf_op jit(solution)/shard_map/all_gather | solution.py:153
  236.1 15.5 %all-gather.14.cloned.1.call-done = bf16[1,1024,1024]{2,1,0:T(8,128)(2,1)} async-done(((bf16[1,256,1024]{2,1,0:T(8,128)(2,1)}), bf16[1,1024,1024]{2,1,0:T(8,128)(2,1)}) %all-gather.14.cloned.1.call-update) | async-done | bytes 2097168 | tf_op jit(solution)/shard_map/all_gather | solution.py:174
  255.5 20.6 %all-gather.12.cloned.1.call-done = bf16[1,1024,1024]{2,1,0:T(8,128)(2,1)} async-done(((bf16[1,256,1024]{2,1,0:T(8,128)(2,1)}), bf16[1,1024,1024]{2,1,0:T(8,128)(2,1)}) %all-gather.12.cloned.1.call-update) | async-done | bytes 2097168 | tf_op jit(solution)/shard_map/all_gather | solution.py:175
  280.1 45.8 %while.30 = (s32[]{:T(128)}, bf16[8,1,256,128]{2,3,1,0:T(8,128)(2,1)S(1)}, f32[8,1,2,256]{3,2,1,0:T(2,128)}, s32[8]{0:T(128)S(1)}, bf16[1,1024,1024]{1,2,0:T(8,1...) while((s32[]{:T(128)}, ...), condition=%wide.region_5.6_spmd.clone.clone, body=%wide.region_2.5_spmd.clone.sunk.clone | while | flops 138149376 | bytes 8804011 | solution.py:192
  332.7 151.0 %all-gather.20.cloned.1.call-done = bf16[1024,5248]{0,1:T(8,128)(2,1)} async-done(((bf16[1024,656]{0,1:T(8,128)(2,1)}), bf16[1024,5248]{0,1:T(8,128)(2,1)}) %all-gather.20.cloned.1.call-update) | async-done | bytes 10747920 | tf_op jit(solution)/shard_map/all_gather | solution.py:152
  511.9 468.5 %while.31 = (s32[]{:T(128)}, f32[8,1,256,128]{2,3,1,0:T(8,128)}, f32[8,1,256,128]{2,3,1,0:T(8,128)}, bf16[8,1,256,128]{2,3,1,0:T(8,128)(2,1)}, s32[8]{0:T(128)S(...) while((s32[]{:T(128)}, f32[8,1,256,128]{2,3,1,0:T(8,128)}, ...), condition=%wide.region_14.15_spmd.clone.clone, body=%wide.region_10.14_spmd.clone.sunk.clone | while | flops 343477248 | bytes 23342488 | solution.py:284
  546.3 21.2 %reduce-scatter.5.cloned.1.call-done = bf16[1,256,128]{1,2,0:T(8,128)(2,1)} async-done(((bf16[1,1024,128]{1,2,0:T(8,128)(2,1)}), bf16[1,256,128]{1,2,0:T(8,128)(2,1)}) %reduce-scatter.5.cloned.1.call-update) | async-done | bytes 65552 | tf_op jit(solution)/shard_map/while/body/eval_jaxpr/reduce_scatter | solution.py:275
  591.2 12.4 %reduce-scatter.3.cloned.1.call-done = bf16[1,256,128]{1,2,0:T(8,128)(2,1)} async-done(((bf16[1,1024,128]{1,2,0:T(8,128)(2,1)}), bf16[1,256,128]{1,2,0:T(8,128)(2,1)}) %reduce-scatter.3.cloned.1.call-update) | async-done | bytes 65552 | tf_op jit(solution)/shard_map/while/body/eval_jaxpr/reduce_scatter | solution.py:269
  605.1 21.1 %reduce-scatter.5.cloned.1.call-done = bf16[1,256,128]{1,2,0:T(8,128)(2,1)} async-done(((bf16[1,1024,128]{1,2,0:T(8,128)(2,1)}), bf16[1,256,128]{1,2,0:T(8,128)(2,1)}) %reduce-scatter.5.cloned.1.call-update) | async-done | bytes 65552 | tf_op jit(solution)/shard_map/while/body/eval_jaxpr/reduce_scatter | solution.py:275
  650.0 12.4 %reduce-scatter.3.cloned.1.call-done = bf16[1,256,128]{1,2,0:T(8,128)(2,1)} async-done(((bf16[1,1024,128]{1,2,0:T(8,128)(2,1)}), bf16[1,256,128]{1,2,0:T(8,128)(2,1)}) %reduce-scatter.3.cloned.1.call-update) | async-done | bytes 65552 | tf_op jit(solution)/shard_map/while/body/eval_jaxpr/reduce_scatter | solution.py:269
  663.9 21.1 %reduce-scatter.5.cloned.1.call-done = bf16[1,256,128]{1,2,0:T(8,128)(2,1)} async-done(((bf16[1,1024,128]{1,2,0:T(8,128)(2,1)}), bf16[1,256,128]{1,2,0:T(8,128)(2,1)}) %reduce-scatter.5.cloned.1.call-update) | async-done | bytes 65552 | tf_op jit(solution)/shard_map/while/body/eval_jaxpr/reduce_scatter | solution.py:275
  708.8 12.4 %reduce-scatter.3.cloned.1.call-done = bf16[1,256,128]{1,2,0:T(8,128)(2,1)} async-done(((bf16[1,1024,128]{1,2,0:T(8,128)(2,1)}), bf16[1,256,128]{1,2,0:T(8,128)(2,1)}) %reduce-scatter.3.cloned.1.call-update) | async-done | bytes 65552 | tf_op jit(solution)/shard_map/while/body/eval_jaxpr/reduce_scatter | solution.py:269
  722.7 21.0 %reduce-scatter.5.cloned.1.call-done = bf16[1,256,128]{1,2,0:T(8,128)(2,1)} async-done(((bf16[1,1024,128]{1,2,0:T(8,128)(2,1)}), bf16[1,256,128]{1,2,0:T(8,128)(2,1)}) %reduce-scatter.5.cloned.1.call-update) | async-done | bytes 65552 | tf_op jit(solution)/shard_map/while/body/eval_jaxpr/reduce_scatter | solution.py:275
  767.4 12.4 %reduce-scatter.3.cloned.1.call-done = bf16[1,256,128]{1,2,0:T(8,128)(2,1)} async-done(((bf16[1,1024,128]{1,2,0:T(8,128)(2,1)}), bf16[1,256,128]{1,2,0:T(8,128)(2,1)}) %reduce-scatter.3.cloned.1.call-update) | async-done | bytes 65552 | tf_op jit(solution)/shard_map/while/body/eval_jaxpr/reduce_scatter | solution.py:269
  781.4 21.0 %reduce-scatter.5.cloned.1.call-done = bf16[1,256,128]{1,2,0:T(8,128)(2,1)} async-done(((bf16[1,1024,128]{1,2,0:T(8,128)(2,1)}), bf16[1,256,128]{1,2,0:T(8,128)(2,1)}) %reduce-scatter.5.cloned.1.call-update) | async-done | bytes 65552 | tf_op jit(solution)/shard_map/while/body/eval_jaxpr/reduce_scatter | solution.py:275
  826.2 12.4 %reduce-scatter.3.cloned.1.call-done = bf16[1,256,128]{1,2,0:T(8,128)(2,1)} async-done(((bf16[1,1024,128]{1,2,0:T(8,128)(2,1)}), bf16[1,256,128]{1,2,0:T(8,128)(2,1)}) %reduce-scatter.3.cloned.1.call-update) | async-done | bytes 65552 | tf_op jit(solution)/shard_map/while/body/eval_jaxpr/reduce_scatter | solution.py:269
  840.1 21.2 %reduce-scatter.5.cloned.1.call-done = bf16[1,256,128]{1,2,0:T(8,128)(2,1)} async-done(((bf16[1,1024,128]{1,2,0:T(8,128)(2,1)}), bf16[1,256,128]{1,2,0:T(8,128)(2,1)}) %reduce-scatter.5.cloned.1.call-update) | async-done | bytes 65552 | tf_op jit(solution)/shard_map/while/body/eval_jaxpr/reduce_scatter | solution.py:275
  884.9 12.4 %reduce-scatter.3.cloned.1.call-done = bf16[1,256,128]{1,2,0:T(8,128)(2,1)} async-done(((bf16[1,1024,128]{1,2,0:T(8,128)(2,1)}), bf16[1,256,128]{1,2,0:T(8,128)(2,1)}) %reduce-scatter.3.cloned.1.call-update) | async-done | bytes 65552 | tf_op jit(solution)/shard_map/while/body/eval_jaxpr/reduce_scatter | solution.py:269
  898.9 21.2 %reduce-scatter.5.cloned.1.call-done = bf16[1,256,128]{1,2,0:T(8,128)(2,1)} async-done(((bf16[1,1024,128]{1,2,0:T(8,128)(2,1)}), bf16[1,256,128]{1,2,0:T(8,128)(2,1)}) %reduce-scatter.5.cloned.1.call-update) | async-done | bytes 65552 | tf_op jit(solution)/shard_map/while/body/eval_jaxpr/reduce_scatter | solution.py:275
  943.8 12.4 %reduce-scatter.3.cloned.1.call-done = bf16[1,256,128]{1,2,0:T(8,128)(2,1)} async-done(((bf16[1,1024,128]{1,2,0:T(8,128)(2,1)}), bf16[1,256,128]{1,2,0:T(8,128)(2,1)}) %reduce-scatter.3.cloned.1.call-update) | async-done | bytes 65552 | tf_op jit(solution)/shard_map/while/body/eval_jaxpr/reduce_scatter | solution.py:269
  957.7 21.2 %reduce-scatter.5.cloned.1.call-done = bf16[1,256,128]{1,2,0:T(8,128)(2,1)} async-done(((bf16[1,1024,128]{1,2,0:T(8,128)(2,1)}), bf16[1,256,128]{1,2,0:T(8,128)(2,1)}) %reduce-scatter.5.cloned.1.call-update) | async-done | bytes 65552 | tf_op jit(solution)/shard_map/while/body/eval_jaxpr/reduce_scatter | solution.py:275
  1007.6 166.9 %all-reduce.7.cloned.1.call-done = (f32[8,16,1024]{2,1,0:T(8,128)}, f32[8,16,3072]{2,1,0:T(8,128)}, f32[8,16,1024]{2,1,0:T(8,128)}, f32[8,16,1024]{2,1,0:T(8,128...) async-done(((f32[8,16,1024]{2,1,0:T(8,128)}, f32[8,16,3072]{2,1,0:T(8,128)}, f32[8,16,1024]{2,1,0:T(8,128)}, ...) | async-done | bytes 8224784 | tf_op jit(solution)/shard_map/psum | solution.py:304
  (517 shorter events, 394.1 us)
Async XLA Ops:
  7.2 112.3 %all-gather.10.cloned.1.call-start = ((), (), s32[]{:S(2)}) async-start(), calls=%async_computation.2 | async-start | bytes 7077888 | tf_op jit(solution)/shard_map/all_gather | solution.py:150
  19.1 136.7 %all-gather.18.cloned.1.call-start = ((), (), s32[]{:S(2)}) async-start(), calls=%async_computation.6 | async-start | bytes 1679360 | tf_op jit(solution)/shard_map/all_gather | solution.py:144
  19.8 208.9 %all-gather.22.cloned.1.call-start = ((), (), s32[]{:S(2)}) async-start(), calls=%async_computation.8 | async-start | bytes 6045696 | tf_op jit(solution)/shard_map/all_gather | solution.py:153
  28.6 222.9 %all-gather.14.cloned.1.call-start = ((), (), s32[]{:S(2)}) async-start(), calls=%async_computation.4 | async-start | bytes 2621440 | tf_op jit(solution)/shard_map/all_gather | solution.py:174
  146.9 129.2 %all-gather.12.cloned.1.call-start = ((), (), s32[]{:S(2)}) async-start(), calls=%async_computation.3 | async-start | bytes 2621440 | tf_op jit(solution)/shard_map/all_gather | solution.py:175
  149.3 179.9 %all-gather.16.cloned.1.call-start = ((), (), s32[]{:S(2)}) async-start(), calls=%async_computation.5 | async-start | bytes 2359296 | tf_op jit(solution)/shard_map/all_gather | solution.py:151
  155.7 327.9 %all-gather.20.cloned.1.call-start = ((), (), s32[]{:S(2)}) async-start(), calls=%async_computation.7 | async-start | bytes 12091392 | tf_op jit(solution)/shard_map/all_gather | solution.py:152
  511.9 32.9 %reduce-scatter.3.cloned.1.call-start = ((), (), s32[]{:S(2)}) async-start(), calls=%async_computation.10 | async-start | bytes 327680 | tf_op jit(solution)/shard_map/while/body/eval_jaxpr/reduce_scatter | solution.py:269
  526.4 41.0 %reduce-scatter.5.cloned.1.call-start = ((), (), s32[]{:S(2)}) async-start(), calls=%async_computation.11 | async-start | bytes 327680 | tf_op jit(solution)/shard_map/while/body/eval_jaxpr/reduce_scatter | solution.py:275
  568.9 34.7 %reduce-scatter.3.cloned.1.call-start = ((), (), s32[]{:S(2)}) async-start(), calls=%async_computation.10 | async-start | bytes 327680 | tf_op jit(solution)/shard_map/while/body/eval_jaxpr/reduce_scatter | solution.py:269
  583.4 42.8 %reduce-scatter.5.cloned.1.call-start = ((), (), s32[]{:S(2)}) async-start(), calls=%async_computation.11 | async-start | bytes 327680 | tf_op jit(solution)/shard_map/while/body/eval_jaxpr/reduce_scatter | solution.py:275
  627.7 34.7 %reduce-scatter.3.cloned.1.call-start = ((), (), s32[]{:S(2)}) async-start(), calls=%async_computation.10 | async-start | bytes 327680 | tf_op jit(solution)/shard_map/while/body/eval_jaxpr/reduce_scatter | solution.py:269
  642.2 42.8 %reduce-scatter.5.cloned.1.call-start = ((), (), s32[]{:S(2)}) async-start(), calls=%async_computation.11 | async-start | bytes 327680 | tf_op jit(solution)/shard_map/while/body/eval_jaxpr/reduce_scatter | solution.py:275
  686.5 34.7 %reduce-scatter.3.cloned.1.call-start = ((), (), s32[]{:S(2)}) async-start(), calls=%async_computation.10 | async-start | bytes 327680 | tf_op jit(solution)/shard_map/while/body/eval_jaxpr/reduce_scatter | solution.py:269
  701.0 42.7 %reduce-scatter.5.cloned.1.call-start = ((), (), s32[]{:S(2)}) async-start(), calls=%async_computation.11 | async-start | bytes 327680 | tf_op jit(solution)/shard_map/while/body/eval_jaxpr/reduce_scatter | solution.py:275
  745.2 34.7 %reduce-scatter.3.cloned.1.call-start = ((), (), s32[]{:S(2)}) async-start(), calls=%async_computation.10 | async-start | bytes 327680 | tf_op jit(solution)/shard_map/while/body/eval_jaxpr/reduce_scatter | solution.py:269
  759.6 42.8 %reduce-scatter.5.cloned.1.call-start = ((), (), s32[]{:S(2)}) async-start(), calls=%async_computation.11 | async-start | bytes 327680 | tf_op jit(solution)/shard_map/while/body/eval_jaxpr/reduce_scatter | solution.py:275
  803.9 34.7 %reduce-scatter.3.cloned.1.call-start = ((), (), s32[]{:S(2)}) async-start(), calls=%async_computation.10 | async-start | bytes 327680 | tf_op jit(solution)/shard_map/while/body/eval_jaxpr/reduce_scatter | solution.py:269
  818.4 42.9 %reduce-scatter.5.cloned.1.call-start = ((), (), s32[]{:S(2)}) async-start(), calls=%async_computation.11 | async-start | bytes 327680 | tf_op jit(solution)/shard_map/while/body/eval_jaxpr/reduce_scatter | solution.py:275
  862.7 34.6 %reduce-scatter.3.cloned.1.call-start = ((), (), s32[]{:S(2)}) async-start(), calls=%async_computation.10 | async-start | bytes 327680 | tf_op jit(solution)/shard_map/while/body/eval_jaxpr/reduce_scatter | solution.py:269
  877.2 42.9 %reduce-scatter.5.cloned.1.call-start = ((), (), s32[]{:S(2)}) async-start(), calls=%async_computation.11 | async-start | bytes 327680 | tf_op jit(solution)/shard_map/while/body/eval_jaxpr/reduce_scatter | solution.py:275
  921.5 34.7 %reduce-scatter.3.cloned.1.call-start = ((), (), s32[]{:S(2)}) async-start(), calls=%async_computation.10 | async-start | bytes 327680 | tf_op jit(solution)/shard_map/while/body/eval_jaxpr/reduce_scatter | solution.py:269
  936.0 42.9 %reduce-scatter.5.cloned.1.call-start = ((), (), s32[]{:S(2)}) async-start(), calls=%async_computation.11 | async-start | bytes 327680 | tf_op jit(solution)/shard_map/while/body/eval_jaxpr/reduce_scatter | solution.py:275
  980.4 194.1 %all-reduce.7.cloned.1.call-start = ((), (), s32[]{:S(2)}) async-start(), calls=%async_computation.9 | async-start | bytes 16515072 | tf_op jit(solution)/shard_map/psum | solution.py:304
  (80 other events, 676.5 us)
Sparse Core Ops, SparseCore 0:
  19.2 100.2 all-gather.9
  121.1 16.6 all-gather.17
  139.8 88.8 all-gather.21
  230.7 20.7 all-gather.13
  253.5 22.5 all-gather.11
  278.0 51.1 all-gather.15
  331.4 152.2 all-gather.19
  526.5 18.2 reduce-scatter.2
  547.4 19.9 reduce-scatter.4
  583.5 20.0 reduce-scatter.2
  606.2 19.9 reduce-scatter.4
  642.3 20.0 reduce-scatter.2
  665.0 19.9 reduce-scatter.4
  701.1 20.0 reduce-scatter.2
  723.7 20.0 reduce-scatter.4
  759.8 20.0 reduce-scatter.2
  782.3 20.0 reduce-scatter.4
  818.5 20.0 reduce-scatter.2
  841.2 20.0 reduce-scatter.4
  877.3 20.0 reduce-scatter.2
  900.0 20.0 reduce-scatter.4
  936.1 20.0 reduce-scatter.2
  958.8 20.0 reduce-scatter.4
  994.2 180.2 all-reduce.6
where the time goes:
time: 1200 us; the launch traced here: 1190 us
  waiting for transfers between devices  760 us (63%)
  matrix products  161 us (13%)
  local copies, waits for them, and re-layouts  125 us (10%)
  other arithmetic  65.6 us (5%)
  blocking collectives  37.7 us (3%)
  loops' own time  27.1 us (2%)
  between operations  15.8 us (1%)
    reduce_scatter x8, waiting for transfers between devices, summed_group(): lax.psum_scatter(grad_value.reshape(seq_count, seq_length, group_width).a...  169 us
    psum x1, waiting for transfers between devices, body(): lax.psum((spread_back(terms[0], onehot), spread_back(terms[1], onehot), s...  167 us
    all_gather x1, waiting for transfers between devices, body(): lax.all_gather(tok_parts[2], 'seq', axis=1, tiled=True)  151 us
    reduce_scatter x8, waiting for transfers between devices, summed_group(): lax.psum_scatter(grad_key.reshape(seq_count, seq_length, group_width).ast...  97.5 us
    all_gather x1, waiting for transfers between devices, body(): lax.all_gather(tok_parts[0], 'seq', axis=1, tiled=True)  75.4 us
    all_gather x1, waiting for transfers between devices, body(): lax.all_gather(tok_parts[3], 'seq', axis=1, tiled=True)  59.1 us
    dynamic_slice x48, local copies, waits for them, and re-layouts, heads_slice(): lax.dynamic_slice_in_dim(source, group_index * group_width, group_width, 2)  48.9 us
    dot_general x8, matrix products, summed_group(): jnp.einsum('shqk,sqhd->skhd', grad_scores, query_part, preferred_element_...  28.5 us
  transfers between devices with their start and end apart: 24, of which 23 were waited for; matrix products, arithmetic and copies ran while one was open for 16% of the time, Pallas kernels for 0%

commit v1 on v0

--- a/solution.py
+++ b/solution.py
@@ -301,7 +301,7 @@
     _, norm_one_back = jax.vjp(lambda field: layer_norm(field, gain_one), inputs)
     input_grad = (grad_mid + norm_one_back(back_norm_one)[0]).astype(jnp.bfloat16)
     terms = (down_qkv, up_qkv, down_out, up_out, down_in, up_in, down_o2, up_o2)
-    summed = lax.psum(
+    partial = lax.psum(
         (
             spread_back(terms[0], onehot),
             spread_back(terms[1], onehot),
@@ -312,8 +312,9 @@
             spread_back(terms[6], onehot),
             spread_back(terms[7], onehot),
         ),
-        ("seq", "tok"),
-    )
+        "tok",
+    )
+    summed = lax.psum(partial, "seq")
     return (
         layer_out,
         input_grad,

time: 1200 us -> 1450 us (1.21)
  waiting for transfers between devices: 760 us -> 1010 us
    psum x0 -> x1, waiting for transfers between devices: none -> 264 us  [body(): summed = lax.psum(partial, 'seq')]
  transfers between devices with their start and end apart: 24 -> 25, of which waited for: 23 -> 24; matrix products, arithmetic and copies ran while one was open for 16% -> 13% of each run, Pallas kernels for 0% -> 0%
where the time goes in v1:
time: 1450 us; the launch traced here: 1440 us
  waiting for transfers between devices  1010 us (70%)
  matrix products  161 us (11%)
  local copies, waits for them, and re-layouts  125 us (9%)
  other arithmetic  65.6 us (5%)
  blocking collectives  37.7 us (3%)
  loops' own time  27.1 us (2%)
  between operations  15.5 us (1%)
    psum x1, waiting for transfers between devices, body(): summed = lax.psum(partial, 'seq')  264 us
    reduce_scatter x8, waiting for transfers between devices, summed_group(): lax.psum_scatter(grad_value.reshape(seq_count, seq_length, group_width).a...  169 us
    psum x1, waiting for transfers between devices, body(): lax.psum((spread_back(terms[0], onehot), spread_back(terms[1], onehot), s...  153 us
    all_gather x1, waiting for transfers between devices, body(): lax.all_gather(tok_parts[2], 'seq', axis=1, tiled=True)  151 us
    reduce_scatter x8, waiting for transfers between devices, summed_group(): lax.psum_scatter(grad_key.reshape(seq_count, seq_length, group_width).ast...  96.9 us
    all_gather x1, waiting for transfers between devices, body(): lax.all_gather(tok_parts[0], 'seq', axis=1, tiled=True)  75.4 us
    all_gather x1, waiting for transfers between devices, body(): lax.all_gather(tok_parts[3], 'seq', axis=1, tiled=True)  59.1 us
    dynamic_slice x48, local copies, waits for them, and re-layouts, heads_slice(): lax.dynamic_slice_in_dim(source, group_index * group_width, group_width, 2)  48.8 us
  transfers between devices with their start and end apart: 25, of which 24 were waited for; matrix products, arithmetic and copies ran while one was open for 13% of the time, Pallas kernels for 0%

profile of v1, /device:TPU:0, one launch (start us, length us, event | category | flops | bytes accessed | tf_op | source)
XLA Modules:
  0.0 1442.7 jit_solution(8183967225230349632)
XLA Ops:
  44.1 75.4 %all-gather.10.cloned.1.call-done = bf16[1024,3072]{1,0:T(8,128)(2,1)} async-done(((bf16[1024,384]{1,0:T(8,128)(2,1)}), bf16[1024,3072]{1,0:T(8,128)(2,1)}) %all-gather.10.cloned.1.call-update) | async-done | bytes 6291472 | tf_op jit(solution)/shard_map/all_gather | solution.py:150
  169.6 59.1 %all-gather.22.cloned.1.call-done = bf16[2624,1024]{1,0:T(8,128)(2,1)} async-done(((bf16[2624,128]{1,0:T(8,128)(2,1)}), bf16[2624,1024]{1,0:T(8,128)(2,1)}) %all-gather.22.cloned.1.call-update) | async-done | bytes 5373968 | tf_op jit(solution)/shard_map/all_gather | solution.py:153
  236.1 15.5 %all-gather.14.cloned.1.call-done = bf16[1,1024,1024]{2,1,0:T(8,128)(2,1)} async-done(((bf16[1,256,1024]{2,1,0:T(8,128)(2,1)}), bf16[1,1024,1024]{2,1,0:T(8,128)(2,1)}) %all-gather.14.cloned.1.call-update) | async-done | bytes 2097168 | tf_op jit(solution)/shard_map/all_gather | solution.py:174
  255.5 20.6 %all-gather.12.cloned.1.call-done = bf16[1,1024,1024]{2,1,0:T(8,128)(2,1)} async-done(((bf16[1,256,1024]{2,1,0:T(8,128)(2,1)}), bf16[1,1024,1024]{2,1,0:T(8,128)(2,1)}) %all-gather.12.cloned.1.call-update) | async-done | bytes 2097168 | tf_op jit(solution)/shard_map/all_gather | solution.py:175
  280.1 45.8 %while.30 = (s32[]{:T(128)}, bf16[8,1,256,128]{2,3,1,0:T(8,128)(2,1)S(1)}, f32[8,1,2,256]{3,2,1,0:T(2,128)}, s32[8]{0:T(128)S(1)}, bf16[1,1024,1024]{1,2,0:T(8,1...) while((s32[]{:T(128)}, ...), condition=%wide.region_5.6_spmd.clone.clone, body=%wide.region_2.5_spmd.clone.sunk.clone | while | flops 138149376 | bytes 8804011 | solution.py:192
  332.7 151.0 %all-gather.20.cloned.1.call-done = bf16[1024,5248]{0,1:T(8,128)(2,1)} async-done(((bf16[1024,656]{0,1:T(8,128)(2,1)}), bf16[1024,5248]{0,1:T(8,128)(2,1)}) %all-gather.20.cloned.1.call-update) | async-done | bytes 10747920 | tf_op jit(solution)/shard_map/all_gather | solution.py:152
  511.9 468.2 %while.31 = (s32[]{:T(128)}, f32[8,1,256,128]{2,3,1,0:T(8,128)}, f32[8,1,256,128]{2,3,1,0:T(8,128)}, bf16[8,1,256,128]{2,3,1,0:T(8,128)(2,1)}, s32[8]{0:T(128)S(...) while((s32[]{:T(128)}, f32[8,1,256,128]{2,3,1,0:T(8,128)}, ...), condition=%wide.region_14.15_spmd.clone.clone, body=%wide.region_10.14_spmd.clone.sunk.clone | while | flops 343477248 | bytes 23342488 | solution.py:284
  546.2 21.2 %reduce-scatter.5.cloned.1.call-done = bf16[1,256,128]{1,2,0:T(8,128)(2,1)} async-done(((bf16[1,1024,128]{1,2,0:T(8,128)(2,1)}), bf16[1,256,128]{1,2,0:T(8,128)(2,1)}) %reduce-scatter.5.cloned.1.call-update) | async-done | bytes 65552 | tf_op jit(solution)/shard_map/while/body/eval_jaxpr/reduce_scatter | solution.py:275
  591.2 12.3 reduce-scatter.3.cloned.1.call-done
  605.0 21.2 %reduce-scatter.5.cloned.1.call-done = bf16[1,256,128]{1,2,0:T(8,128)(2,1)} async-done(((bf16[1,1024,128]{1,2,0:T(8,128)(2,1)}), bf16[1,256,128]{1,2,0:T(8,128)(2,1)}) %reduce-scatter.5.cloned.1.call-update) | async-done | bytes 65552 | tf_op jit(solution)/shard_map/while/body/eval_jaxpr/reduce_scatter | solution.py:275
  650.0 12.3 reduce-scatter.3.cloned.1.call-done
  663.8 21.2 %reduce-scatter.5.cloned.1.call-done = bf16[1,256,128]{1,2,0:T(8,128)(2,1)} async-done(((bf16[1,1024,128]{1,2,0:T(8,128)(2,1)}), bf16[1,256,128]{1,2,0:T(8,128)(2,1)}) %reduce-scatter.5.cloned.1.call-update) | async-done | bytes 65552 | tf_op jit(solution)/shard_map/while/body/eval_jaxpr/reduce_scatter | solution.py:275
  708.8 12.3 reduce-scatter.3.cloned.1.call-done
  722.6 21.0 %reduce-scatter.5.cloned.1.call-done = bf16[1,256,128]{1,2,0:T(8,128)(2,1)} async-done(((bf16[1,1024,128]{1,2,0:T(8,128)(2,1)}), bf16[1,256,128]{1,2,0:T(8,128)(2,1)}) %reduce-scatter.5.cloned.1.call-update) | async-done | bytes 65552 | tf_op jit(solution)/shard_map/while/body/eval_jaxpr/reduce_scatter | solution.py:275
  767.4 12.3 reduce-scatter.3.cloned.1.call-done
  781.3 21.0 %reduce-scatter.5.cloned.1.call-done = bf16[1,256,128]{1,2,0:T(8,128)(2,1)} async-done(((bf16[1,1024,128]{1,2,0:T(8,128)(2,1)}), bf16[1,256,128]{1,2,0:T(8,128)(2,1)}) %reduce-scatter.5.cloned.1.call-update) | async-done | bytes 65552 | tf_op jit(solution)/shard_map/while/body/eval_jaxpr/reduce_scatter | solution.py:275
  826.0 12.3 reduce-scatter.3.cloned.1.call-done
  839.9 21.2 %reduce-scatter.5.cloned.1.call-done = bf16[1,256,128]{1,2,0:T(8,128)(2,1)} async-done(((bf16[1,1024,128]{1,2,0:T(8,128)(2,1)}), bf16[1,256,128]{1,2,0:T(8,128)(2,1)}) %reduce-scatter.5.cloned.1.call-update) | async-done | bytes 65552 | tf_op jit(solution)/shard_map/while/body/eval_jaxpr/reduce_scatter | solution.py:275
  884.8 12.3 reduce-scatter.3.cloned.1.call-done
  898.7 21.2 %reduce-scatter.5.cloned.1.call-done = bf16[1,256,128]{1,2,0:T(8,128)(2,1)} async-done(((bf16[1,1024,128]{1,2,0:T(8,128)(2,1)}), bf16[1,256,128]{1,2,0:T(8,128)(2,1)}) %reduce-scatter.5.cloned.1.call-update) | async-done | bytes 65552 | tf_op jit(solution)/shard_map/while/body/eval_jaxpr/reduce_scatter | solution.py:275
  943.6 12.3 reduce-scatter.3.cloned.1.call-done
  957.4 21.2 %reduce-scatter.5.cloned.1.call-done = bf16[1,256,128]{1,2,0:T(8,128)(2,1)} async-done(((bf16[1,1024,128]{1,2,0:T(8,128)(2,1)}), bf16[1,256,128]{1,2,0:T(8,128)(2,1)}) %reduce-scatter.5.cloned.1.call-update) | async-done | bytes 65552 | tf_op jit(solution)/shard_map/while/body/eval_jaxpr/reduce_scatter | solution.py:275
  993.8 153.1 %all-reduce.11.cloned.1.call-done = (f32[8,16,1024]{2,1,0:T(8,128)}, f32[8,16,3072]{2,1,0:T(8,128)}, f32[8,16,1024]{2,1,0:T(8,128)}, f32[8,16,1024]{2,1,0:T(8,12...) async-done(((f32[8,16,1024]{2,1,0:T(8,128)}, f32[8,16,3072]{2,1,0:T(8,128)}, f32[8,16,1024]{2,1,0:T(8,128)}, ...) | async-done | bytes 8224784 | tf_op jit(solution)/shard_map/psum | solution.py:304
  1160.0 264.2 %all-reduce.9.cloned.1.call-done = (f32[8,16,1024]{2,1,0:T(8,128)}, f32[8,16,3072]{2,1,0:T(8,128)}, f32[8,16,1024]{2,1,0:T(8,128)}, f32[8,16,1024]{2,1,0:T(8,128...) async-done(((f32[8,16,1024]{2,1,0:T(8,128)}, f32[8,16,3072]{2,1,0:T(8,128)}, f32[8,16,1024]{2,1,0:T(8,128)}, ...) | async-done | bytes 8224784 | tf_op jit(solution)/shard_map/psum | solution.py:317
  (520 shorter events, 405.6 us)
Async XLA Ops:
  7.2 112.3 %all-gather.10.cloned.1.call-start = ((), (), s32[]{:S(2)}) async-start(), calls=%async_computation.2 | async-start | bytes 7077888 | tf_op jit(solution)/shard_map/all_gather | solution.py:150
  19.1 136.8 %all-gather.18.cloned.1.call-start = ((), (), s32[]{:S(2)}) async-start(), calls=%async_computation.6 | async-start | bytes 1679360 | tf_op jit(solution)/shard_map/all_gather | solution.py:144
  19.8 208.9 %all-gather.22.cloned.1.call-start = ((), (), s32[]{:S(2)}) async-start(), calls=%async_computation.8 | async-start | bytes 6045696 | tf_op jit(solution)/shard_map/all_gather | solution.py:153
  28.7 222.9 %all-gather.14.cloned.1.call-start = ((), (), s32[]{:S(2)}) async-start(), calls=%async_computation.4 | async-start | bytes 2621440 | tf_op jit(solution)/shard_map/all_gather | solution.py:174
  147.0 129.2 %all-gather.12.cloned.1.call-start = ((), (), s32[]{:S(2)}) async-start(), calls=%async_computation.3 | async-start | bytes 2621440 | tf_op jit(solution)/shard_map/all_gather | solution.py:175
  149.3 179.9 %all-gather.16.cloned.1.call-start = ((), (), s32[]{:S(2)}) async-start(), calls=%async_computation.5 | async-start | bytes 2359296 | tf_op jit(solution)/shard_map/all_gather | solution.py:151
  155.8 327.9 %all-gather.20.cloned.1.call-start = ((), (), s32[]{:S(2)}) async-start(), calls=%async_computation.7 | async-start | bytes 12091392 | tf_op jit(solution)/shard_map/all_gather | solution.py:152
  526.4 41.0 %reduce-scatter.5.cloned.1.call-start = ((), (), s32[]{:S(2)}) async-start(), calls=%async_computation.12 | async-start | bytes 327680 | tf_op jit(solution)/shard_map/while/body/eval_jaxpr/reduce_scatter | solution.py:275
  568.9 34.7 %reduce-scatter.3.cloned.1.call-start = ((), (), s32[]{:S(2)}) async-start(), calls=%async_computation.11 | async-start | bytes 327680 | tf_op jit(solution)/shard_map/while/body/eval_jaxpr/reduce_scatter | solution.py:269
  583.4 42.8 %reduce-scatter.5.cloned.1.call-start = ((), (), s32[]{:S(2)}) async-start(), calls=%async_computation.12 | async-start | bytes 327680 | tf_op jit(solution)/shard_map/while/body/eval_jaxpr/reduce_scatter | solution.py:275
  627.7 34.7 %reduce-scatter.3.cloned.1.call-start = ((), (), s32[]{:S(2)}) async-start(), calls=%async_computation.11 | async-start | bytes 327680 | tf_op jit(solution)/shard_map/while/body/eval_jaxpr/reduce_scatter | solution.py:269
  642.2 42.8 %reduce-scatter.5.cloned.1.call-start = ((), (), s32[]{:S(2)}) async-start(), calls=%async_computation.12 | async-start | bytes 327680 | tf_op jit(solution)/shard_map/while/body/eval_jaxpr/reduce_scatter | solution.py:275
  686.5 34.6 %reduce-scatter.3.cloned.1.call-start = ((), (), s32[]{:S(2)}) async-start(), calls=%async_computation.11 | async-start | bytes 327680 | tf_op jit(solution)/shard_map/while/body/eval_jaxpr/reduce_scatter | solution.py:269
  701.0 42.7 %reduce-scatter.5.cloned.1.call-start = ((), (), s32[]{:S(2)}) async-start(), calls=%async_computation.12 | async-start | bytes 327680 | tf_op jit(solution)/shard_map/while/body/eval_jaxpr/reduce_scatter | solution.py:275
  745.1 34.7 %reduce-scatter.3.cloned.1.call-start = ((), (), s32[]{:S(2)}) async-start(), calls=%async_computation.11 | async-start | bytes 327680 | tf_op jit(solution)/shard_map/while/body/eval_jaxpr/reduce_scatter | solution.py:269
  759.6 42.7 %reduce-scatter.5.cloned.1.call-start = ((), (), s32[]{:S(2)}) async-start(), calls=%async_computation.12 | async-start | bytes 327680 | tf_op jit(solution)/shard_map/while/body/eval_jaxpr/reduce_scatter | solution.py:275
  803.8 34.6 %reduce-scatter.3.cloned.1.call-start = ((), (), s32[]{:S(2)}) async-start(), calls=%async_computation.11 | async-start | bytes 327680 | tf_op jit(solution)/shard_map/while/body/eval_jaxpr/reduce_scatter | solution.py:269
  818.2 42.8 %reduce-scatter.5.cloned.1.call-start = ((), (), s32[]{:S(2)}) async-start(), calls=%async_computation.12 | async-start | bytes 327680 | tf_op jit(solution)/shard_map/while/body/eval_jaxpr/reduce_scatter | solution.py:275
  862.5 34.7 %reduce-scatter.3.cloned.1.call-start = ((), (), s32[]{:S(2)}) async-start(), calls=%async_computation.11 | async-start | bytes 327680 | tf_op jit(solution)/shard_map/while/body/eval_jaxpr/reduce_scatter | solution.py:269
  877.0 42.8 %reduce-scatter.5.cloned.1.call-start = ((), (), s32[]{:S(2)}) async-start(), calls=%async_computation.12 | async-start | bytes 327680 | tf_op jit(solution)/shard_map/while/body/eval_jaxpr/reduce_scatter | solution.py:275
  921.3 34.6 %reduce-scatter.3.cloned.1.call-start = ((), (), s32[]{:S(2)}) async-start(), calls=%async_computation.11 | async-start | bytes 327680 | tf_op jit(solution)/shard_map/while/body/eval_jaxpr/reduce_scatter | solution.py:269
  935.8 42.9 %reduce-scatter.5.cloned.1.call-start = ((), (), s32[]{:S(2)}) async-start(), calls=%async_computation.12 | async-start | bytes 327680 | tf_op jit(solution)/shard_map/while/body/eval_jaxpr/reduce_scatter | solution.py:275
  980.1 166.8 %all-reduce.11.cloned.1.call-start = ((), (), s32[]{:S(2)}) async-start(), calls=%async_computation.10 | async-start | bytes 16515072 | tf_op jit(solution)/shard_map/psum | solution.py:304
  993.6 430.7 %all-reduce.9.cloned.1.call-start = ((), (), s32[]{:S(2)}) async-start(), calls=%async_computation.9 | async-start | bytes 16515072 | tf_op jit(solution)/shard_map/psum | solution.py:317
  (81 other events, 709.0 us)
Sparse Core Ops, SparseCore 0:
  19.2 100.2 all-gather.9
  139.9 88.8 all-gather.21
  230.7 20.7 all-gather.13
  253.5 22.5 all-gather.11
  278.0 51.0 all-gather.15
  331.4 152.2 all-gather.19
  526.5 18.1 reduce-scatter.2
  547.3 20.0 reduce-scatter.4
  583.5 19.9 reduce-scatter.2
  606.1 20.0 reduce-scatter.4
  642.3 19.9 reduce-scatter.2
  664.9 20.0 reduce-scatter.4
  701.1 19.9 reduce-scatter.2
  723.6 20.0 reduce-scatter.4
  759.7 19.9 reduce-scatter.2
  782.2 20.0 reduce-scatter.4
  818.3 19.9 reduce-scatter.2
  841.0 20.0 reduce-scatter.4
  877.1 19.9 reduce-scatter.2
  899.8 20.0 reduce-scatter.4
  935.9 19.9 reduce-scatter.2
  958.5 20.0 reduce-scatter.4
  993.7 153.1 all-reduce.10
  1153.2 271.0 all-reduce.8
  (1 shorter events, 16.6 us)
